TPU v7x, 32 devices: a whole 2x2x4 slice. The times are simulated.
32 devices in a mesh: row: 16 (over z, y, x), col: 2 (over core).
Axes of the slice: x: 2, y: 2, z: 4, core: 2. Of those that a mesh axis runs over, the one named last changes fastest.
Arguments:
- latent: bfloat16 [6144, 512], P('row', 'col'), may hold values from -6 to 6
- w_kv: bfloat16 [512, 8192], P('row', 'col'), may hold values from -0.25 to 0.25
- queries: bfloat16 [6144, 4096], P('row', 'col'), may hold values from -240 to 240
- w_out: bfloat16 [4096, 7168], P('row', 'col'), may hold values from -0.09375 to 0.09375
Outputs:
- mixed: bfloat16 [6144, 7168], P('row', 'col')
All inputs are finite; a program needn't handle non-finite values.
Results may differ from a plain program's by a relative error of at most 0.012.
The roundings to bfloat16 on the way count: a program that leaves them out, or rounds other values in their place, can miss the bound.
Values may be sent and summed in bfloat16 or wider, within the bound.
No kernel may reach another device: no remote copies, remote signals or barrier semaphores. Data moves between devices by JAX's collectives and lax.ppermute only.
A program may use at most 128 MiB of HBM per device.

v0:
```python
import math
import jax
import jax.numpy as jnp
from jax import lax
from jax.sharding import PartitionSpec as P

HEAD = 128
NEG_FILL = -1e30


def per_device(latent, w_kv, queries, w_out):
    row_count = lax.axis_size("row")
    tok_rows = latent.shape[0]
    per_col = queries.shape[1] // HEAD
    quarters = row_count // per_col
    stripe = tok_rows // quarters
    my_row = lax.axis_index("row")
    quarter = my_row // per_col
    pair_width = 2 * HEAD
    latent_rows = lax.all_gather(latent, "col", axis=1, tiled=True)
    columns = latent_rows
    summed = jnp.dot(
        columns, lax.all_gather(w_kv, "row", axis=0, tiled=True), preferred_element_type=jnp.float32
    )
    expanded = summed.astype(jnp.bfloat16).reshape(tok_rows, per_col, pair_width).transpose(1, 0, 2)
    copies = jnp.broadcast_to(expanded[None], (quarters, per_col, tok_rows, pair_width))
    copies = copies.reshape(row_count, tok_rows, pair_width)
    keyvals = lax.all_to_all(copies, "row", split_axis=0, concat_axis=1, tiled=True).reshape(
        row_count * tok_rows, pair_width
    )
    split_queries = queries.reshape(quarters, stripe, per_col, HEAD).transpose(0, 2, 1, 3)
    split_queries = split_queries.reshape(row_count, stripe, HEAD)
    my_queries = lax.all_to_all(
        split_queries, "row", split_axis=0, concat_axis=1, tiled=True
    ).reshape(row_count * stripe, HEAD)
    sources_per_block = row_count
    for candidate in range(1, row_count + 1):
        if row_count % candidate == 0 and candidate * stripe >= 256:
            sources_per_block = candidate
            break
    block_rows = sources_per_block * stripe
    key_span = sources_per_block * tok_rows
    key_block = math.gcd(key_span, 512)
    score_scale = HEAD ** (-0.5)
    pieces_done = []
    for block_index in range(row_count // sources_per_block):
        query_block = my_queries[block_index * block_rows : (block_index + 1) * block_rows]
        local_rows = jnp.arange(block_rows, dtype=jnp.int32)
        query_pos = (
            (block_index * sources_per_block + local_rows // stripe) * tok_rows
            + quarter * stripe
            + local_rows % stripe
        )

        def key_turn(key_index, carry, query_block=query_block, query_pos=query_pos):
            running_max, running_sum, weighted = carry
            first_key = key_index * key_block
            pairs = lax.dynamic_slice_in_dim(keyvals, first_key, key_block, 0)
            scores = (
                lax.dot_general(
                    query_block,
                    pairs[:, :HEAD],
                    (((1,), (1,)), ((), ())),
                    preferred_element_type=jnp.float32,
                )
                * score_scale
            )
            key_pos = first_key + jnp.arange(key_block, dtype=jnp.int32)
            allowed = key_pos[None, :] <= query_pos[:, None]
            scores = jnp.where(allowed, scores, NEG_FILL)
            new_max = jnp.maximum(running_max, jnp.max(scores, axis=1))
            rescale = jnp.exp(running_max - new_max)
            weights = jnp.where(allowed, jnp.exp(scores - new_max[:, None]), 0.0)
            running_sum = running_sum * rescale + jnp.sum(weights, axis=1)
            weighted = weighted * rescale[:, None] + jnp.dot(
                weights.astype(jnp.bfloat16), pairs[:, HEAD:], preferred_element_type=jnp.float32
            )
            return (new_max, running_sum, weighted)

        starting = (
            jnp.full((block_rows,), NEG_FILL, jnp.float32),
            jnp.zeros((block_rows,), jnp.float32),
            jnp.zeros((block_rows, HEAD), jnp.float32),
        )
        last_pos = (
            ((block_index + 1) * sources_per_block - 1) * tok_rows + quarter * stripe + stripe - 1
        )
        key_steps = (last_pos + key_block) // key_block
        final_max, final_sum, final_weighted = lax.fori_loop(0, key_steps, key_turn, starting)
        pieces_done.append((final_weighted / final_sum[:, None]).astype(jnp.bfloat16))
    attended = jnp.concatenate(pieces_done, axis=0)
    returned = lax.all_to_all(
        attended.reshape(row_count, stripe, HEAD), "row", split_axis=0, concat_axis=0, tiled=True
    )
    attn_tokens = (
        returned.reshape(quarters, per_col, stripe, HEAD)
        .transpose(0, 2, 1, 3)
        .reshape(tok_rows, per_col * HEAD)
    )
    full_features = lax.all_gather(attn_tokens, "col", axis=1, tiled=True)
    columns = full_features
    mixed = jnp.dot(
        columns,
        lax.all_gather(w_out, "row", axis=0, tiled=True),
        preferred_element_type=jnp.float32,
    )
    return mixed.astype(jnp.bfloat16)


def solution(mesh):
    in_specs = (P("row", "col"), P("row", "col"), P("row", "col"), P("row", "col"))
    out_specs = P("row", "col")
    return jax.shard_map(
        per_device, mesh=mesh, in_specs=in_specs, out_specs=out_specs, check_vma=False
    )
```

profile of v0, /device:TPU:0, one launch (start us, length us, event | category | flops | bytes accessed | tf_op | source)
XLA Modules:
  0.0 2180.4 jit_solution(16351844525132143396)
XLA Ops:
  7.3 2.6 copy.44
  9.9 8.3 all-to-all-start.1
  18.2 2.1 all_gather.12
  20.3 83.3 %all-gather.4.cloned.1.call-done = bf16[512,4096]{1,0:T(8,128)(2,1)} async-done(((bf16[32,4096]{1,0:T(8,128)(2,1)}), bf16[512,4096]{1,0:T(8,128)(2,1)}) %all-gather.4.cloned.1.call-update) | async-done | bytes 4194320 | tf_op jit(solution)/shard_map/all_gather | solution.py:23
  103.6 4.0 convolution_convert_fusion.1
  107.6 2.0 copy.64
  110.7 4.2 all-to-all-start
  115.5 2.5 slice_bitcast_fusion
  140.6 35.0 %all-to-all-done = bf16[16,384,256]{2,1,0:T(8,128)(2,1)S(1)} async-done(((bf16[16,384,256]{2,1,0:T(8,128)(2,1)}), bf16[16,384,256]{2,1,0:T(8,128)(2,1)S(1)}, u32[]{:S(2)}, u32[]{:S(2)}) %all-to-all-start) | async-done | bytes 3145760 | tf_op jit(solution)/shard_map/all_to_all | solution.py:28
  176.2 10.4 while.240
  188.0 26.5 %while.241 = (s32[]{:T(128)}, f32[384]{0:T(512)S(1)}, f32[384]{0:T(512)}, f32[384,128]{1,0:T(8,128)}, s32[]{:T(128)}, /*index=5*/bf16[6144,256]{1,0:T(8,128)(2,1...) while((s32[]{:T(128)}, f32[384]{0:T(512)S(1)}, ...), condition=%wide.region_7.8_spmd.clone, body=%wide.region_4.7_spmd.clone.sunk | while | flops 25859080 | bytes 1183975 | solution.py:89
  215.1 31.5 %while.242 = (s32[]{:T(128)}, f32[384]{0:T(512)S(1)}, f32[384]{0:T(512)}, f32[384,128]{1,0:T(8,128)S(1)}, s32[]{:T(128)}, /*index=5*/bf16[6144,256]{1,0:T(8,128)...) while((s32[]{:T(128)}, f32[384]{0:T(512)S(1)}, ...), condition=%wide.region_11.12_spmd.clone, body=%wide.region_8.11_spmd.clone.sunk | while | flops 25859080 | bytes 1183975 | solution.py:89
  247.9 53.3 %while.243 = (s32[]{:T(128)}, f32[384]{0:T(512)S(1)}, f32[384]{0:T(512)}, f32[384,128]{1,0:T(8,128)}, s32[]{:T(128)}, /*index=5*/bf16[6144,256]{1,0:T(8,128)(2,1...) while((s32[]{:T(128)}, f32[384]{0:T(512)S(1)}, ...), condition=%wide.region_15.16_spmd.clone, body=%wide.region_12.15_spmd.clone.sunk | while | flops 25859080 | bytes 1183975 | solution.py:89
  250.5 1.9 convolution_add_fusion.35
  254.9 1.9 convolution_add_fusion.35
  259.3 1.9 convolution_add_fusion.35
  263.8 1.9 convolution_add_fusion.35
  268.2 1.9 convolution_add_fusion.35
  272.7 1.9 convolution_add_fusion.35
  277.1 1.9 convolution_add_fusion.35
  281.5 1.9 convolution_add_fusion.35
  286.0 1.9 convolution_add_fusion.35
  290.4 1.9 convolution_add_fusion.35
  294.9 1.9 convolution_add_fusion.35
  299.3 1.9 convolution_add_fusion.35
  301.8 50.9 %while.244 = (s32[]{:T(128)}, f32[384]{0:T(512)S(1)}, f32[384]{0:T(512)}, f32[384,128]{1,0:T(8,128)S(1)}, s32[]{:T(128)}, /*index=5*/bf16[6144,256]{1,0:T(8,128)...) while((s32[]{:T(128)}, f32[384]{0:T(512)S(1)}, ...), condition=%wide.region_19.20_spmd.clone, body=%wide.region_16.19_spmd.clone.sunk | while | flops 25859080 | bytes 1183975 | solution.py:89
  354.0 79.4 %while.245 = (s32[]{:T(128)}, f32[384]{0:T(512)S(1)}, f32[384]{0:T(512)}, f32[384,128]{1,0:T(8,128)}, s32[]{:T(128)}, /*index=5*/bf16[6144,256]{1,0:T(8,128)(2,1...) while((s32[]{:T(128)}, f32[384]{0:T(512)S(1)}, ...), condition=%wide.region_23.24_spmd.clone, body=%wide.region_20.23_spmd.clone.sunk | while | flops 25859080 | bytes 1183975 | solution.py:89
  434.1 71.6 %while.246 = (s32[]{:T(128)}, f32[384]{0:T(512)S(1)}, f32[384]{0:T(512)}, f32[384,128]{1,0:T(8,128)S(1)}, s32[]{:T(128)}, /*index=5*/bf16[6144,256]{1,0:T(8,128)...) while((s32[]{:T(128)}, f32[384]{0:T(512)S(1)}, ...), condition=%wide.region_27.28_spmd.clone, body=%wide.region_24.27_spmd.clone.sunk | while | flops 25859080 | bytes 1183975 | solution.py:89
  507.1 106.1 %while.247 = (s32[]{:T(128)}, f32[384]{0:T(512)S(1)}, f32[384]{0:T(512)}, f32[384,128]{1,0:T(8,128)}, s32[]{:T(128)}, /*index=5*/bf16[6144,256]{1,0:T(8,128)(2,1...) while((s32[]{:T(128)}, f32[384]{0:T(512)S(1)}, ...), condition=%wide.region_31.32_spmd.clone, body=%wide.region_28.31_spmd.clone.sunk | while | flops 25859080 | bytes 1183975 | solution.py:89
  509.6 1.9 convolution_add_fusion.39
  514.0 1.9 convolution_add_fusion.39
  518.4 1.9 convolution_add_fusion.39
  522.8 1.9 convolution_add_fusion.39
  527.3 1.9 convolution_add_fusion.39
  531.7 1.9 convolution_add_fusion.39
  536.1 1.9 convolution_add_fusion.39
  540.5 1.9 convolution_add_fusion.39
  544.9 1.9 convolution_add_fusion.39
  549.4 1.9 convolution_add_fusion.39
  553.8 1.9 convolution_add_fusion.39
  558.2 1.9 convolution_add_fusion.39
  562.6 1.9 convolution_add_fusion.39
  567.0 1.9 convolution_add_fusion.39
  571.5 1.9 convolution_add_fusion.39
  575.9 1.9 convolution_add_fusion.39
  580.3 1.9 convolution_add_fusion.39
  584.7 1.9 convolution_add_fusion.39
  589.1 1.9 convolution_add_fusion.39
  593.6 1.9 convolution_add_fusion.39
  598.0 1.9 convolution_add_fusion.39
  602.4 1.9 convolution_add_fusion.39
  606.8 1.9 convolution_add_fusion.39
  613.8 94.2 %while.248 = (s32[]{:T(128)}, f32[384]{0:T(512)S(1)}, f32[384]{0:T(512)}, f32[384,128]{1,0:T(8,128)S(1)}, s32[]{:T(128)}, /*index=5*/bf16[6144,256]{1,0:T(8,128)...) while((s32[]{:T(128)}, f32[384]{0:T(512)S(1)}, ...), condition=%wide.region_35.36_spmd.clone, body=%wide.region_32.35_spmd.clone.sunk | while | flops 25859080 | bytes 1183975 | solution.py:89
  709.4 132.6 %while.249 = (s32[]{:T(128)}, f32[384]{0:T(512)S(1)}, f32[384]{0:T(512)}, f32[384,128]{1,0:T(8,128)}, s32[]{:T(128)}, /*index=5*/bf16[6144,256]{1,0:T(8,128)(2,1...) while((s32[]{:T(128)}, f32[384]{0:T(512)S(1)}, ...), condition=%wide.region_39.40_spmd.clone, body=%wide.region_36.39_spmd.clone.sunk | while | flops 25859080 | bytes 1183975 | solution.py:89
  842.6 116.8 %while.250 = (s32[]{:T(128)}, f32[384]{0:T(512)S(1)}, f32[384]{0:T(512)}, f32[384,128]{1,0:T(8,128)S(1)}, s32[]{:T(128)}, /*index=5*/bf16[6144,256]{1,0:T(8,128)...) while((s32[]{:T(128)}, f32[384]{0:T(512)S(1)}, ...), condition=%wide.region_43.44_spmd.clone, body=%wide.region_40.43_spmd.clone.sunk | while | flops 25859080 | bytes 1183975 | solution.py:89
  960.8 158.0 %while.251 = (s32[]{:T(128)}, f32[384]{0:T(512)S(1)}, f32[384]{0:T(512)}, f32[384,128]{1,0:T(8,128)}, s32[]{:T(128)}, /*index=5*/bf16[6144,256]{1,0:T(8,128)(2,1...) while((s32[]{:T(128)}, f32[384]{0:T(512)S(1)}, ...), condition=%wide.region_47.48_spmd.clone, body=%wide.region_44.47_spmd.clone.sunk | while | flops 25859080 | bytes 1183975 | solution.py:89
  1119.4 134.8 %while.252 = (s32[]{:T(128)}, f32[384]{0:T(512)S(1)}, f32[384]{0:T(512)}, f32[384,128]{1,0:T(8,128)S(1)}, s32[]{:T(128)}, /*index=5*/bf16[6144,256]{1,0:T(8,128)...) while((s32[]{:T(128)}, f32[384]{0:T(512)S(1)}, ...), condition=%wide.region_51.52_spmd.clone, body=%wide.region_48.51_spmd.clone.sunk | while | flops 25859080 | bytes 1183975 | solution.py:89
  1255.5 185.7 %while.253 = (s32[]{:T(128)}, f32[384]{0:T(512)S(1)}, f32[384]{0:T(512)}, f32[384,128]{1,0:T(8,128)}, s32[]{:T(128)}, /*index=5*/bf16[6144,256]{1,0:T(8,128)(2,1...) while((s32[]{:T(128)}, f32[384]{0:T(512)S(1)}, ...), condition=%wide.region_55.56_spmd.clone, body=%wide.region_52.55_spmd.clone.sunk | while | flops 25859080 | bytes 1183975 | solution.py:89
  1441.8 152.4 %while.254 = (s32[]{:T(128)}, f32[384]{0:T(512)S(1)}, f32[384]{0:T(512)}, f32[384,128]{1,0:T(8,128)S(1)}, s32[]{:T(128)}, /*index=5*/bf16[6144,256]{1,0:T(8,128)...) while((s32[]{:T(128)}, f32[384]{0:T(512)S(1)}, ...), condition=%wide.region_59.60_spmd.clone, body=%wide.region_56.59_spmd.clone.sunk | while | flops 25859080 | bytes 1183975 | solution.py:89
  1594.9 169.7 %while.255 = (s32[]{:T(128)}, f32[384]{0:T(512)S(1)}, f32[384]{0:T(512)}, f32[384,128]{1,0:T(8,128)S(1)}, s32[]{:T(128)}, /*index=5*/bf16[6144,256]{1,0:T(8,128)...) while((s32[]{:T(128)}, f32[384]{0:T(512)S(1)}, ...), condition=%wide.region_63.64_spmd.clone, body=%wide.region_60.63_spmd.clone.sunk | while | flops 25859080 | bytes 1183975 | solution.py:89
  1777.3 50.8 %all_to_all.23 = bf16[16,384,128]{2,1,0:T(8,128)(2,1)S(1)} all-to-all(bf16[16,384,128]{2,1,0:T(8,128)(2,1)S(1)} %bitcast.171), channel_id=1, replica_groups=mesh['row'=16,'col'=2] {'row'}, dimensions={0} | all-to-all | bytes 3145728 | tf_op jit(solution)/shard_map/all_to_all | solution.py:92
  1830.5 9.9 all-gather.6.cloned.1.call-done
  1840.4 314.2 %all-gather.8.cloned.1.call-done = bf16[4096,3584]{1,0:T(8,128)(2,1)} async-done(((bf16[256,3584]{1,0:T(8,128)(2,1)}), bf16[4096,3584]{1,0:T(8,128)(2,1)}) %all-gather.8.cloned.1.call-update) | async-done | bytes 29360144 | tf_op jit(solution)/shard_map/all_gather | solution.py:104
  2154.5 19.3 convolution_convert_fusion
  (4173 shorter events, 1541.3 us)
Async XLA Ops:
  6.5 97.1 %all-gather.4.cloned.1.call-start = ((), (), s32[]{:S(2)}) async-start(), calls=%async_computation.3 | async-start | bytes 4456448 | tf_op jit(solution)/shard_map/all_gather | solution.py:23
  7.3 11.0 copy-start.14
  9.9 99.7 %all-to-all-start.1 = ((bf16[16,384,128]{1,2,0:T(8,128)(2,1)}), bf16[16,384,128]{1,2,0:T(8,128)(2,1)S(1)}, u32[]{:S(2)}, u32[]{:S(2)}) async-start(bf16[16,384,128]{1,2,0:T(8,128)(2,1)} %bitcast.4), calls=%async_computation.1 | async-start | bytes 3145728 | tf_op jit(solution)/shard_map/all_to_all | solution.py:33
  110.7 64.9 %all-to-all-start = ((bf16[16,384,256]{2,1,0:T(8,128)(2,1)}), bf16[16,384,256]{2,1,0:T(8,128)(2,1)S(1)}, u32[]{:S(2)}, u32[]{:S(2)}) async-start(bf16[16,384,256]{2,1,0:T(8,128)(2,1)} %bitcast.167), calls=%async_computation | async-start | bytes 6291456 | tf_op jit(solution)/shard_map/all_to_all | solution.py:28
  115.0 1725.4 %all-gather.6.cloned.1.call-start = ((), (), s32[]{:S(2)}) async-start(), calls=%async_computation.4 | async-start | bytes 4718592 | tf_op jit(solution)/shard_map/all_gather | solution.py:100
  247.9 2.5 copy-start.18
  252.4 2.5 copy-start.18
  256.8 2.5 copy-start.18
  261.3 2.5 copy-start.18
  265.7 2.5 copy-start.18
  270.1 2.5 copy-start.18
  279.0 2.5 copy-start.18
  283.4 2.5 copy-start.18
  287.9 2.5 copy-start.18
  296.8 2.5 copy-start.18
  709.4 2.5 copy-start.24
  713.8 2.5 copy-start.24
  718.2 2.5 copy-start.24
  722.6 2.5 copy-start.24
  727.0 2.5 copy-start.24
  731.5 2.5 copy-start.24
  735.9 2.5 copy-start.24
  740.3 2.5 copy-start.24
  744.7 2.5 copy-start.24
  749.2 2.5 copy-start.24
  753.6 2.5 copy-start.24
  758.0 2.5 copy-start.24
  762.4 2.5 copy-start.24
  766.8 2.5 copy-start.24
  771.3 2.5 copy-start.24
  775.7 2.5 copy-start.24
  780.1 2.5 copy-start.24
  784.5 2.5 copy-start.24
  788.9 2.5 copy-start.24
  793.4 2.5 copy-start.24
  797.8 2.5 copy-start.24
  802.2 2.5 copy-start.24
  806.6 2.5 copy-start.24
  811.0 2.5 copy-start.24
  815.5 2.5 copy-start.24
  819.9 2.5 copy-start.24
  824.3 2.5 copy-start.24
  828.7 2.5 copy-start.24
  833.2 2.5 copy-start.24
  837.6 2.5 copy-start.24
  1255.5 2.5 copy-start.28
  1286.5 2.5 copy-start.28
  1290.9 2.5 copy-start.28
  1295.3 2.5 copy-start.28
  1326.3 2.5 copy-start.28
  1330.7 2.5 copy-start.28
  1335.1 2.5 copy-start.28
  1339.6 2.5 copy-start.28
  1764.7 11.0 copy-start.6
  1764.7 11.8 copy-start.7
  1764.7 11.8 copy-start.32
  1764.7 12.0 copy-start.9
  1764.7 12.0 copy-start.33
  1764.7 12.1 copy-start.10
  1764.7 12.1 copy-start.34
  1764.7 12.3 copy-start.12
  1764.7 12.3 copy-start.35
  1764.7 12.4 copy-start.31
  1829.7 324.8 %all-gather.8.cloned.1.call-start = ((), (), s32[]{:S(2)}) async-start(), calls=%async_computation.5 | async-start | bytes 31195136 | tf_op jit(solution)/shard_map/all_gather | solution.py:104
  (369 other events, 908.9 us)
Sparse Core Ops, SparseCore 0:
  10.1 93.4 all-gather.3
  1829.9 10.4 all-gather.5
  1843.1 311.4 all-gather.7
where the time goes:
time: 2210 us; the launch traced here: 2180 us
  matrix products  1010 us (46%)
  other arithmetic  573 us (26%)
  waiting for transfers between devices  444 us (20%)
  blocking collectives  52.9 us (2%)
  local copies, waits for them, and re-layouts  49.7 us (2%)
    dot_general x408, matrix products, key_turn(): jnp.dot(weights.astype(jnp.bfloat16), pairs[:, HEAD:], preferred_element_...  542 us
    add x408, other arithmetic, key_turn(): running_sum = running_sum * rescale + jnp.sum(weights, axis=1)  511 us
    dot_general x408, matrix products, key_turn(): lax.dot_general(query_block, pairs[:, :HEAD], (((1,), (1,)), ((), ())), p...  449 us
    all_gather x1, waiting for transfers between devices, per_device(): lax.all_gather(w_out, 'row', axis=0, tiled=True)  314 us
    all_gather x1, waiting for transfers between devices, per_device(): lax.all_gather(w_kv, 'row', axis=0, tiled=True)  83.3 us
    all_to_all x1, blocking collectives, per_device(): lax.all_to_all(attended.reshape(row_count, stripe, HEAD), 'row', split_ax...  50.8 us

commit v1 on v0

--- a/solution.py
+++ b/solution.py
@@ -6,6 +6,18 @@
 
 HEAD = 128
 NEG_FILL = -1e30
+
+
+def gather_around(array, axis, dim):
+    ways, here, turn = (lax.axis_size(axis), lax.axis_index(axis), array.shape[dim])
+    shape = [n * ways if d == dim else n for d, n in enumerate(array.shape)]
+    full = lax.dynamic_update_slice_in_dim(
+        jnp.zeros(shape, array.dtype), array, here * turn, axis=dim
+    )
+    for far in range(1, ways):
+        array = lax.ppermute(array, axis, [(d, (d + 1) % ways) for d in range(ways)])
+        full = lax.dynamic_update_slice_in_dim(full, array, (here - far) % ways * turn, axis=dim)
+    return full
 
 
 def per_device(latent, w_kv, queries, w_out):
@@ -99,11 +111,7 @@
     )
     full_features = lax.all_gather(attn_tokens, "col", axis=1, tiled=True)
     columns = full_features
-    mixed = jnp.dot(
-        columns,
-        lax.all_gather(w_out, "row", axis=0, tiled=True),
-        preferred_element_type=jnp.float32,
-    )
+    mixed = jnp.dot(columns, gather_around(w_out, "row", 0), preferred_element_type=jnp.float32)
     return mixed.astype(jnp.bfloat16)
 
 

time: 2210 us -> 2370 us (1.072)
  the two profiles are of different devices: /device:TPU:0 before, /device:TPU:8 now
where the time goes in v1:
time: 2370 us; the launch traced here: 2340 us
  matrix products  1020 us (43%)
  other arithmetic  582 us (25%)
  waiting for transfers between devices  528 us (22%)
  local copies, waits for them, and re-layouts  100 us (4%)
  starting transfers between devices  75.5 us (3%)
    dot_general x408, matrix products, key_turn(): jnp.dot(weights.astype(jnp.bfloat16), pairs[:, HEAD:], preferred_element_...  550 us
    add x408, other arithmetic, key_turn(): running_sum = running_sum * rescale + jnp.sum(weights, axis=1)  510 us
    ppermute x15, waiting for transfers between devices, gather_around(): lax.ppermute(array, axis, [(d, (d + 1) % ways) for d in range(ways)])  454 us
    dot_general x408, matrix products, key_turn(): lax.dot_general(query_block, pairs[:, :HEAD], (((1,), (1,)), ((), ())), p...  449 us
    all_to_all x1, waiting for transfers between devices, per_device(): lax.all_to_all(split_queries, 'row', split_axis=0, concat_axis=1, tiled=T...  63.8 us
    ppermute x15, starting transfers between devices, gather_around(): lax.ppermute(array, axis, [(d, (d + 1) % ways) for d in range(ways)])  50.7 us

profile of v1, /device:TPU:8, one launch (start us, length us, event | category | flops | bytes accessed | tf_op | source)
XLA Modules:
  0.0 2344.1 jit_solution(15669312930092674267)
XLA Ops:
  8.8 47.9 %collective-permute-done = bf16[256,3584]{1,0:T(8,128)(2,1)S(1)} collective-permute-done((bf16[256,3584]{1,0:T(8,128)(2,1)}, bf16[256,3584]{1,0:T(8,128)(2,1)S(1)}, u32[]{:S(2)}, u32[]{:S(2)}) %collective-permute-start) | collective-permute-done | bytes 1835040 | tf_op jit(solution)/shard_map/ppermute | solution.py:18
  56.7 70.7 %collective-permute-done.1 = bf16[256,3584]{1,0:T(8,128)(2,1)} collective-permute-done((bf16[256,3584]{1,0:T(8,128)(2,1)S(1)}, bf16[256,3584]{1,0:T(8,128)(2,1)}, u32[]{:S(2)}, u32[]{:S(2)}) %collective-permute-start.1) | collective-permute-done | bytes 1835040 | tf_op jit(solution)/shard_map/ppermute | solution.py:18
  127.4 2.6 copy.44
  130.0 13.7 all-to-all-start.1
  143.6 37.5 %collective-permute-done.2 = bf16[256,3584]{1,0:T(8,128)(2,1)} collective-permute-done((bf16[256,3584]{1,0:T(8,128)(2,1)}, bf16[256,3584]{1,0:T(8,128)(2,1)}, u32[]{:S(2)}, u32[]{:S(2)}) %collective-permute-start.2) | collective-permute-done | bytes 1835040 | tf_op jit(solution)/shard_map/ppermute | solution.py:18
  181.1 2.1 all_gather.9
  183.2 4.0 convolution_convert_fusion.1
  187.2 2.0 copy.64
  189.2 63.8 %all-to-all-done.1 = bf16[16,384,128]{1,2,0:T(8,128)(2,1)S(1)} async-done(((bf16[16,384,128]{1,2,0:T(8,128)(2,1)}), bf16[16,384,128]{1,2,0:T(8,128)(2,1)S(1)}, u32[]{:S(2)}, u32[]{:S(2)}) %all-to-all-start.1) | async-done | bytes 1572896 | tf_op jit(solution)/shard_map/all_to_all | solution.py:45
  254.1 5.4 all-to-all-start
  261.1 94.1 %collective-permute-done.4 = bf16[256,3584]{1,0:T(8,128)(2,1)S(1)} collective-permute-done((bf16[256,3584]{1,0:T(8,128)(2,1)}, bf16[256,3584]{1,0:T(8,128)(2,1)S(1)}, u32[]{:S(2)}, u32[]{:S(2)}) %collective-permute-start.4) | collective-permute-done | bytes 1835040 | tf_op jit(solution)/shard_map/ppermute | solution.py:18
  356.5 43.8 %collective-permute-done.5 = bf16[256,3584]{1,0:T(8,128)(2,1)} collective-permute-done((bf16[256,3584]{1,0:T(8,128)(2,1)S(1)}, bf16[256,3584]{1,0:T(8,128)(2,1)}, u32[]{:S(2)}, u32[]{:S(2)}) %collective-permute-start.5) | collective-permute-done | bytes 1835040 | tf_op jit(solution)/shard_map/ppermute | solution.py:18
  400.3 9.8 broadcast_in_dim.180
  437.2 2.8 constant_dynamic-update-slice_fusion.12
  440.0 4.9 collective-permute-done.6
  444.9 7.3 collective-permute-start.7
  452.8 10.6 while.240
  464.8 26.3 %while.241 = (s32[]{:T(128)}, f32[384]{0:T(512)S(1)}, f32[384]{0:T(512)}, f32[384,128]{1,0:T(8,128)}, s32[]{:T(128)}, /*index=5*/bf16[6144,256]{1,0:T(8,128)(2,1...) while((s32[]{:T(128)}, f32[384]{0:T(512)S(1)}, ...), condition=%wide.region_7.8_spmd.clone, body=%wide.region_4.7_spmd.clone.sunk | while | flops 25859080 | bytes 1183975 | solution.py:101
  491.8 31.6 %while.242 = (s32[]{:T(128)}, f32[384]{0:T(512)S(1)}, f32[384]{0:T(512)}, f32[384,128]{1,0:T(8,128)S(1)}, s32[]{:T(128)}, /*index=5*/bf16[6144,256]{1,0:T(8,128)...) while((s32[]{:T(128)}, f32[384]{0:T(512)S(1)}, ...), condition=%wide.region_11.12_spmd.clone, body=%wide.region_8.11_spmd.clone.sunk | while | flops 25859080 | bytes 1183975 | solution.py:101
  524.7 53.1 %while.243 = (s32[]{:T(128)}, f32[384]{0:T(512)S(1)}, f32[384]{0:T(512)}, f32[384,128]{1,0:T(8,128)}, s32[]{:T(128)}, /*index=5*/bf16[6144,256]{1,0:T(8,128)(2,1...) while((s32[]{:T(128)}, f32[384]{0:T(512)S(1)}, ...), condition=%wide.region_15.16_spmd.clone, body=%wide.region_12.15_spmd.clone.sunk | while | flops 25859080 | bytes 1183975 | solution.py:101
  578.4 53.0 %while.244 = (s32[]{:T(128)}, f32[384]{0:T(512)S(1)}, f32[384]{0:T(512)}, f32[384,128]{1,0:T(8,128)S(1)}, s32[]{:T(128)}, /*index=5*/bf16[6144,256]{1,0:T(8,128)...) while((s32[]{:T(128)}, f32[384]{0:T(512)S(1)}, ...), condition=%wide.region_19.20_spmd.clone, body=%wide.region_16.19_spmd.clone.sunk | while | flops 25859080 | bytes 1183975 | solution.py:101
  632.7 78.0 %while.245 = (s32[]{:T(128)}, f32[384]{0:T(512)S(1)}, f32[384]{0:T(512)}, f32[384,128]{1,0:T(8,128)}, s32[]{:T(128)}, /*index=5*/bf16[6144,256]{1,0:T(8,128)(2,1...) while((s32[]{:T(128)}, f32[384]{0:T(512)S(1)}, ...), condition=%wide.region_23.24_spmd.clone, body=%wide.region_20.23_spmd.clone.sunk | while | flops 25859080 | bytes 1183975 | solution.py:101
  711.3 74.2 %while.246 = (s32[]{:T(128)}, f32[384]{0:T(512)S(1)}, f32[384]{0:T(512)}, f32[384,128]{1,0:T(8,128)S(1)}, s32[]{:T(128)}, /*index=5*/bf16[6144,256]{1,0:T(8,128)...) while((s32[]{:T(128)}, f32[384]{0:T(512)S(1)}, ...), condition=%wide.region_27.28_spmd.clone, body=%wide.region_24.27_spmd.clone.sunk | while | flops 25859080 | bytes 1183975 | solution.py:101
  786.8 105.8 %while.247 = (s32[]{:T(128)}, f32[384]{0:T(512)S(1)}, f32[384]{0:T(512)}, f32[384,128]{1,0:T(8,128)}, s32[]{:T(128)}, /*index=5*/bf16[6144,256]{1,0:T(8,128)(2,1...) while((s32[]{:T(128)}, f32[384]{0:T(512)S(1)}, ...), condition=%wide.region_31.32_spmd.clone, body=%wide.region_28.31_spmd.clone.sunk | while | flops 25859080 | bytes 1183975 | solution.py:101
  893.2 91.9 %while.248 = (s32[]{:T(128)}, f32[384]{0:T(512)S(1)}, f32[384]{0:T(512)}, f32[384,128]{1,0:T(8,128)S(1)}, s32[]{:T(128)}, /*index=5*/bf16[6144,256]{1,0:T(8,128)...) while((s32[]{:T(128)}, f32[384]{0:T(512)S(1)}, ...), condition=%wide.region_35.36_spmd.clone, body=%wide.region_32.35_spmd.clone.sunk | while | flops 25859080 | bytes 1183975 | solution.py:101
  986.5 132.9 %while.249 = (s32[]{:T(128)}, f32[384]{0:T(512)S(1)}, f32[384]{0:T(512)}, f32[384,128]{1,0:T(8,128)}, s32[]{:T(128)}, /*index=5*/bf16[6144,256]{1,0:T(8,128)(2,1...) while((s32[]{:T(128)}, f32[384]{0:T(512)S(1)}, ...), condition=%wide.region_39.40_spmd.clone, body=%wide.region_36.39_spmd.clone.sunk | while | flops 25859080 | bytes 1183975 | solution.py:101
  1120.0 116.6 %while.250 = (s32[]{:T(128)}, f32[384]{0:T(512)S(1)}, f32[384]{0:T(512)}, f32[384,128]{1,0:T(8,128)S(1)}, s32[]{:T(128)}, /*index=5*/bf16[6144,256]{1,0:T(8,128)...) while((s32[]{:T(128)}, f32[384]{0:T(512)S(1)}, ...), condition=%wide.region_43.44_spmd.clone, body=%wide.region_40.43_spmd.clone.sunk | while | flops 25859080 | bytes 1183975 | solution.py:101
  1237.9 159.4 %while.251 = (s32[]{:T(128)}, f32[384]{0:T(512)S(1)}, f32[384]{0:T(512)}, f32[384,128]{1,0:T(8,128)}, s32[]{:T(128)}, /*index=5*/bf16[6144,256]{1,0:T(8,128)(2,1...) while((s32[]{:T(128)}, f32[384]{0:T(512)S(1)}, ...), condition=%wide.region_47.48_spmd.clone, body=%wide.region_44.47_spmd.clone.sunk | while | flops 25859080 | bytes 1183975 | solution.py:101
  1398.0 137.7 %while.252 = (s32[]{:T(128)}, f32[384]{0:T(512)S(1)}, f32[384]{0:T(512)}, f32[384,128]{1,0:T(8,128)S(1)}, s32[]{:T(128)}, /*index=5*/bf16[6144,256]{1,0:T(8,128)...) while((s32[]{:T(128)}, f32[384]{0:T(512)S(1)}, ...), condition=%wide.region_51.52_spmd.clone, body=%wide.region_48.51_spmd.clone.sunk | while | flops 25859080 | bytes 1183975 | solution.py:101
  1536.9 180.7 %while.253 = (s32[]{:T(128)}, f32[384]{0:T(512)S(1)}, f32[384]{0:T(512)}, f32[384,128]{1,0:T(8,128)}, s32[]{:T(128)}, /*index=5*/bf16[6144,256]{1,0:T(8,128)(2,1...) while((s32[]{:T(128)}, f32[384]{0:T(512)S(1)}, ...), condition=%wide.region_55.56_spmd.clone, body=%wide.region_52.55_spmd.clone.sunk | while | flops 25859080 | bytes 1183975 | solution.py:101
  1543.6 1.9 convolution_add_fusion.45
  1547.9 1.9 convolution_add_fusion.45
  1582.3 1.9 convolution_add_fusion.45
  1586.7 1.9 convolution_add_fusion.45
  1591.0 1.9 convolution_add_fusion.45
  1625.4 1.9 convolution_add_fusion.45
  1629.7 1.9 convolution_add_fusion.45
  1664.1 1.9 convolution_add_fusion.45
  1668.4 1.9 convolution_add_fusion.45
  1672.7 1.9 convolution_add_fusion.45
  1707.1 1.9 convolution_add_fusion.45
  1717.7 4.2 collective-permute-start.8
  1722.5 159.3 %while.254 = (s32[]{:T(128)}, f32[384]{0:T(512)S(1)}, f32[384]{0:T(512)}, f32[384,128]{1,0:T(8,128)S(1)}, s32[]{:T(128)}, /*index=5*/bf16[6144,256]{1,0:T(8,128)...) while((s32[]{:T(128)}, f32[384]{0:T(512)S(1)}, ...), condition=%wide.region_59.60_spmd.clone, body=%wide.region_56.59_spmd.clone.sunk | while | flops 25859080 | bytes 1183975 | solution.py:101
  1881.8 36.1 %collective-permute-start.9 = (bf16[256,3584]{1,0:T(8,128)(2,1)}, bf16[256,3584]{1,0:T(8,128)(2,1)}, u32[]{:S(2)}, u32[]{:S(2)}) collective-permute-start(bf16[256,3584]{1,0:T(8,128)(2,1)} %collective-permute-done.8), channel_id=1, source_target_pairs={{0,2},{2,4},{4,6},{6,8},{8,10},{10,12},{12,14},{14,16},{16,18},{18... | collective-permute-start | bytes 5505032 | tf_op jit(solution)/shard_map/ppermute | solution.py:18
  1918.5 170.5 %while.255 = (s32[]{:T(128)}, f32[384]{0:T(512)S(1)}, f32[384]{0:T(512)}, f32[384,128]{1,0:T(8,128)S(1)}, s32[]{:T(128)}, /*index=5*/bf16[6144,256]{1,0:T(8,128)...) while((s32[]{:T(128)}, f32[384]{0:T(512)S(1)}, ...), condition=%wide.region_63.64_spmd.clone, body=%wide.region_60.63_spmd.clone.sunk | while | flops 25859080 | bytes 1183975 | solution.py:101
  2103.0 34.5 %collective-permute-done.10 = bf16[256,3584]{1,0:T(8,128)(2,1)} collective-permute-done((bf16[256,3584]{1,0:T(8,128)(2,1)}, bf16[256,3584]{1,0:T(8,128)(2,1)}, u32[]{:S(2)}, u32[]{:S(2)}) %collective-permute-start.10) | collective-permute-done | bytes 1835040 | tf_op jit(solution)/shard_map/ppermute | solution.py:18
  2146.1 5.7 all-to-all-start.2
  2151.8 37.0 %collective-permute-done.11 = bf16[256,3584]{1,0:T(8,128)(2,1)} collective-permute-done((bf16[256,3584]{1,0:T(8,128)(2,1)}, bf16[256,3584]{1,0:T(8,128)(2,1)}, u32[]{:S(2)}, u32[]{:S(2)}) %collective-permute-start.11) | collective-permute-done | bytes 1835040 | tf_op jit(solution)/shard_map/ppermute | solution.py:18
  2188.9 2.9 constant_dynamic-update-slice_fusion.11
  2191.7 2.8 constant_dynamic-update-slice_fusion.10
  2195.9 2.8 constant_dynamic-update-slice_fusion.8
  2198.8 49.2 %collective-permute-done.12 = bf16[256,3584]{1,0:T(8,128)(2,1)} collective-permute-done((bf16[256,3584]{1,0:T(8,128)(2,1)}, bf16[256,3584]{1,0:T(8,128)(2,1)}, u32[]{:S(2)}, u32[]{:S(2)}) %collective-permute-start.12) | collective-permute-done | bytes 1835040 | tf_op jit(solution)/shard_map/ppermute | solution.py:18
  2248.0 2.8 constant_dynamic-update-slice_fusion.7
  2250.8 2.8 constant_dynamic-update-slice_fusion.6
  2253.7 9.5 all-to-all-done.2
  2264.7 2.9 constant_dynamic-update-slice_fusion.5
  2267.6 2.9 constant_dynamic-update-slice_fusion.4
  2270.5 21.0 collective-permute-done.13
  2291.5 2.9 constant_dynamic-update-slice_fusion.3
  2294.4 2.9 constant_dynamic-update-slice_fusion.2
  2297.3 2.9 constant_dynamic-update-slice_fusion.1
  2300.2 2.9 constant_dynamic-update-slice_fusion
  2303.1 13.7 collective-permute-done.14
  2318.1 19.2 convolution_convert_fusion
  (4230 shorter events, 1615.4 us)
Async XLA Ops:
  6.5 176.7 %all-gather.3.cloned.1.call-start = ((), (), s32[]{:S(2)}) async-start(), calls=%async_computation.3 | async-start | bytes 4456448 | tf_op jit(solution)/shard_map/all_gather | solution.py:35
  7.3 173.9 %copy-start.20 = (bf16[384,256]{1,0:T(8,128)(2,1)S(1)}, bf16[384,256]{1,0:T(8,128)(2,1)}, u32[]{:S(2)}) copy-start(bf16[384,256]{1,0:T(8,128)(2,1)} %param.36) | copy-start | bytes 589828
  7.3 49.4 %collective-permute-start = (bf16[256,3584]{1,0:T(8,128)(2,1)}, bf16[256,3584]{1,0:T(8,128)(2,1)S(1)}, u32[]{:S(2)}, u32[]{:S(2)}) collective-permute-start(bf16[256,3584]{1,0:T(8,128)(2,1)} %param.39), channel_id=1, source_target_pairs={{0,2},{2,4},{4,6},{6,8},{8,10},{10,12},{12,14},{14,16},{16,18},{18... | collective-permute-start | bytes 5505032 | tf_op jit(solution)/shard_map/ppermute | solution.py:18
  56.7 73.3 %copy-start.18 = (bf16[256,3584]{1,0:T(8,128)(2,1)}, bf16[256,3584]{1,0:T(8,128)(2,1)S(1)}, u32[]{:S(2)}) copy-start(bf16[256,3584]{1,0:T(8,128)(2,1)S(1)} %collective-permute-done) | copy-start | bytes 5505028
  56.7 70.7 %collective-permute-start.1 = (bf16[256,3584]{1,0:T(8,128)(2,1)S(1)}, bf16[256,3584]{1,0:T(8,128)(2,1)}, u32[]{:S(2)}, u32[]{:S(2)}) collective-permute-start(bf16[256,3584]{1,0:T(8,128)(2,1)S(1)} %collective-permute-done), channel_id=1, source_target_pairs={{0,2},{2,4},{4,6},{6,8},{8,10},{10,12},{12,14},{14,16},{16,18},{18... | collective-permute-start | bytes 5505032 | tf_op jit(solution)/shard_map/ppermute | solution.py:18
  127.4 53.8 %collective-permute-start.2 = (bf16[256,3584]{1,0:T(8,128)(2,1)}, bf16[256,3584]{1,0:T(8,128)(2,1)}, u32[]{:S(2)}, u32[]{:S(2)}) collective-permute-start(bf16[256,3584]{1,0:T(8,128)(2,1)} %collective-permute-done.1), channel_id=1, source_target_pairs={{0,2},{2,4},{4,6},{6,8},{8,10},{10,12},{12,14},{14,16},{16,18},{18... | collective-permute-start | bytes 5505032 | tf_op jit(solution)/shard_map/ppermute | solution.py:18
  130.0 123.0 %all-to-all-start.1 = ((bf16[16,384,128]{1,2,0:T(8,128)(2,1)}), bf16[16,384,128]{1,2,0:T(8,128)(2,1)S(1)}, u32[]{:S(2)}, u32[]{:S(2)}) async-start(bf16[16,384,128]{1,2,0:T(8,128)(2,1)} %bitcast.4), calls=%async_computation.1 | async-start | bytes 3145728 | tf_op jit(solution)/shard_map/all_to_all | solution.py:45
  181.1 78.4 %collective-permute-start.3 = (bf16[256,3584]{1,0:T(8,128)(2,1)}, bf16[256,3584]{1,0:T(8,128)(2,1)}, u32[]{:S(2)}, u32[]{:S(2)}) collective-permute-start(bf16[256,3584]{1,0:T(8,128)(2,1)} %collective-permute-done.2), channel_id=1, source_target_pairs={{0,2},{2,4},{4,6},{6,8},{8,10},{10,12},{12,14},{14,16},{16,18},{18... | collective-permute-start | bytes 5505032 | tf_op jit(solution)/shard_map/ppermute | solution.py:18
  254.1 198.1 %all-to-all-start = ((bf16[16,384,256]{2,1,0:T(8,128)(2,1)}), bf16[16,384,256]{2,1,0:T(8,128)(2,1)S(1)}, u32[]{:S(2)}, u32[]{:S(2)}) async-start(bf16[16,384,256]{2,1,0:T(8,128)(2,1)} %bitcast.167), calls=%async_computation | async-start | bytes 6291456 | tf_op jit(solution)/shard_map/all_to_all | solution.py:40
  259.5 95.6 %collective-permute-start.4 = (bf16[256,3584]{1,0:T(8,128)(2,1)}, bf16[256,3584]{1,0:T(8,128)(2,1)S(1)}, u32[]{:S(2)}, u32[]{:S(2)}) collective-permute-start(bf16[256,3584]{1,0:T(8,128)(2,1)} %collective-permute-done.3), channel_id=1, source_target_pairs={{0,2},{2,4},{4,6},{6,8},{8,10},{10,12},{12,14},{14,16},{16,18},{18... | collective-permute-start | bytes 5505032 | tf_op jit(solution)/shard_map/ppermute | solution.py:18
  356.5 43.8 %collective-permute-start.5 = (bf16[256,3584]{1,0:T(8,128)(2,1)S(1)}, bf16[256,3584]{1,0:T(8,128)(2,1)}, u32[]{:S(2)}, u32[]{:S(2)}) collective-permute-start(bf16[256,3584]{1,0:T(8,128)(2,1)S(1)} %collective-permute-done.4), channel_id=1, source_target_pairs={{0,2},{2,4},{4,6},{6,8},{8,10},{10,12},{12,14},{14,16},{16,18},{18... | collective-permute-start | bytes 5505032 | tf_op jit(solution)/shard_map/ppermute | solution.py:18
  400.3 44.7 %collective-permute-start.6 = (bf16[256,3584]{1,0:T(8,128)(2,1)}, bf16[256,3584]{1,0:T(8,128)(2,1)}, u32[]{:S(2)}, u32[]{:S(2)}) collective-permute-start(bf16[256,3584]{1,0:T(8,128)(2,1)} %collective-permute-done.5), channel_id=1, source_target_pairs={{0,2},{2,4},{4,6},{6,8},{8,10},{10,12},{12,14},{14,16},{16,18},{18... | collective-permute-start | bytes 5505032 | tf_op jit(solution)/shard_map/ppermute | solution.py:18
  400.3 9.8 copy-start.15
  410.1 3.5 copy-start.14
  444.9 1272.7 %collective-permute-start.7 = (bf16[256,3584]{1,0:T(8,128)(2,1)}, bf16[256,3584]{1,0:T(8,128)(2,1)}, u32[]{:S(2)}, u32[]{:S(2)}) collective-permute-start(bf16[256,3584]{1,0:T(8,128)(2,1)} %collective-permute-done.6), channel_id=1, source_target_pairs={{0,2},{2,4},{4,6},{6,8},{8,10},{10,12},{12,14},{14,16},{16,18},{18... | collective-permute-start | bytes 5505032 | tf_op jit(solution)/shard_map/ppermute | solution.py:18
  1717.7 164.1 %collective-permute-start.8 = (bf16[256,3584]{1,0:T(8,128)(2,1)}, bf16[256,3584]{1,0:T(8,128)(2,1)}, u32[]{:S(2)}, u32[]{:S(2)}) collective-permute-start(bf16[256,3584]{1,0:T(8,128)(2,1)} %collective-permute-done.7), channel_id=1, source_target_pairs={{0,2},{2,4},{4,6},{6,8},{8,10},{10,12},{12,14},{14,16},{16,18},{18... | collective-permute-start | bytes 5505032 | tf_op jit(solution)/shard_map/ppermute | solution.py:18
  1881.8 36.8 %copy-start.11 = (f32[384,128]{1,0:T(8,128)}, f32[384,128]{1,0:T(8,128)S(1)}, u32[]{:S(2)}) copy-start(f32[384,128]{1,0:T(8,128)S(1)} %get-tuple-element.737) | copy-start | bytes 589828
  1881.8 207.3 %collective-permute-start.9 = (bf16[256,3584]{1,0:T(8,128)(2,1)}, bf16[256,3584]{1,0:T(8,128)(2,1)}, u32[]{:S(2)}, u32[]{:S(2)}) collective-permute-start(bf16[256,3584]{1,0:T(8,128)(2,1)} %collective-permute-done.8), channel_id=1, source_target_pairs={{0,2},{2,4},{4,6},{6,8},{8,10},{10,12},{12,14},{14,16},{16,18},{18... | collective-permute-start | bytes 5505032 | tf_op jit(solution)/shard_map/ppermute | solution.py:18
  1922.1 2.5 copy-start.36
  1925.6 2.5 copy-start.36
  1943.4 2.5 copy-start.36
  1946.9 2.5 copy-start.36
  1950.5 2.5 copy-start.36
  1954.0 2.5 copy-start.36
  1957.6 2.5 copy-start.36
  1971.8 2.5 copy-start.36
  1975.4 2.5 copy-start.36
  1978.9 2.5 copy-start.36
  1982.5 2.5 copy-start.36
  1986.0 2.5 copy-start.36
  1989.6 2.5 copy-start.36
  2003.8 2.5 copy-start.36
  2007.3 2.5 copy-start.36
  2010.9 2.5 copy-start.36
  2014.4 2.5 copy-start.36
  2018.0 2.5 copy-start.36
  2021.5 2.5 copy-start.36
  2035.8 2.5 copy-start.36
  2039.3 2.5 copy-start.36
  2042.9 2.5 copy-start.36
  2046.4 2.5 copy-start.36
  2053.5 2.5 copy-start.36
  2071.3 2.5 copy-start.36
  2074.8 2.5 copy-start.36
  2078.4 2.5 copy-start.36
  2085.5 2.5 copy-start.36
  2089.0 51.8 %copy-start.6 = (f32[384,128]{1,0:T(8,128)S(1)}, f32[384,128]{1,0:T(8,128)}, u32[]{:S(2)}) copy-start(f32[384,128]{1,0:T(8,128)} %copy-done.5) | copy-start | bytes 589828
  2089.0 53.2 %copy-start.7 = (f32[384,128]{1,0:T(8,128)S(1)}, f32[384,128]{1,0:T(8,128)}, u32[]{:S(2)}) copy-start(f32[384,128]{1,0:T(8,128)} %get-tuple-element.731) | copy-start | bytes 589828
  2089.0 53.2 %copy-start.38 = (f32[384]{0:T(512)S(1)}, f32[384]{0:T(512)}, u32[]{:S(2)}) copy-start(f32[384]{0:T(512)} %get-tuple-element.732) | copy-start | bytes 4612
  2089.1 54.0 %copy-start.9 = (f32[384,128]{1,0:T(8,128)S(1)}, f32[384,128]{1,0:T(8,128)}, u32[]{:S(2)}) copy-start(f32[384,128]{1,0:T(8,128)} %copy-done.8) | copy-start | bytes 589828
  2089.1 54.0 %copy-start.39 = (f32[384]{0:T(512)S(1)}, f32[384]{0:T(512)}, u32[]{:S(2)}) copy-start(f32[384]{0:T(512)} %get-tuple-element.734) | copy-start | bytes 4612
  2089.1 54.7 %copy-start.10 = (f32[384,128]{1,0:T(8,128)S(1)}, f32[384,128]{1,0:T(8,128)}, u32[]{:S(2)}) copy-start(f32[384,128]{1,0:T(8,128)} %get-tuple-element.735) | copy-start | bytes 589828
  2089.1 54.7 %copy-start.40 = (f32[384]{0:T(512)S(1)}, f32[384]{0:T(512)}, u32[]{:S(2)}) copy-start(f32[384]{0:T(512)} %get-tuple-element.736) | copy-start | bytes 4612
  2089.1 55.5 %copy-start.12 = (f32[384,128]{1,0:T(8,128)S(1)}, f32[384,128]{1,0:T(8,128)}, u32[]{:S(2)}) copy-start(f32[384,128]{1,0:T(8,128)} %copy-done.11) | copy-start | bytes 589828
  2089.1 55.5 %copy-start.41 = (f32[384]{0:T(512)S(1)}, f32[384]{0:T(512)}, u32[]{:S(2)}) copy-start(f32[384]{0:T(512)} %get-tuple-element.738) | copy-start | bytes 4612
  2089.1 56.2 %copy-start.37 = (f32[384]{0:T(512)S(1)}, f32[384]{0:T(512)}, u32[]{:S(2)}) copy-start(f32[384]{0:T(512)} %get-tuple-element.740) | copy-start | bytes 4612
  2089.1 48.3 %collective-permute-start.10 = (bf16[256,3584]{1,0:T(8,128)(2,1)}, bf16[256,3584]{1,0:T(8,128)(2,1)}, u32[]{:S(2)}, u32[]{:S(2)}) collective-permute-start(bf16[256,3584]{1,0:T(8,128)(2,1)} %collective-permute-done.9), channel_id=1, source_target_pairs={{0,2},{2,4},{4,6},{6,8},{8,10},{10,12},{12,14},{14,16},{16,18},{18... | collective-permute-start | bytes 5505032 | tf_op jit(solution)/shard_map/ppermute | solution.py:18
  2137.4 51.4 %collective-permute-start.11 = (bf16[256,3584]{1,0:T(8,128)(2,1)}, bf16[256,3584]{1,0:T(8,128)(2,1)}, u32[]{:S(2)}, u32[]{:S(2)}) collective-permute-start(bf16[256,3584]{1,0:T(8,128)(2,1)} %collective-permute-done.10), channel_id=1, source_target_pairs={{0,2},{2,4},{4,6},{6,8},{8,10},{10,12},{12,14},{14,16},{16,18},{18... | collective-permute-start | bytes 5505032 | tf_op jit(solution)/shard_map/ppermute | solution.py:18
  2146.1 117.0 %all-to-all-start.2 = ((bf16[16,384,128]{2,1,0:T(8,128)(2,1)}), bf16[16,384,128]{2,1,0:T(8,128)(2,1)S(1)}, u32[]{:S(2)}, u32[]{:S(2)}) async-start(bf16[16,384,128]{2,1,0:T(8,128)(2,1)} %bitcast.21), calls=%async_computation.2 | async-start | bytes 3145728 | tf_op jit(solution)/shard_map/all_to_all | solution.py:104
  2151.8 166.3 %all-gather.5.cloned.1.call-start = ((), (), s32[]{:S(2)}) async-start(), calls=%async_computation.4 | async-start | bytes 4718592 | tf_op jit(solution)/shard_map/all_gather | solution.py:112
  2151.8 42.8 %copy-start.17 = (bf16[256,3584]{1,0:T(8,128)(2,1)S(1)}, bf16[256,3584]{1,0:T(8,128)(2,1)}, u32[]{:S(2)}) copy-start(bf16[256,3584]{1,0:T(8,128)(2,1)} %copy-done.16) | copy-start | bytes 5505028
  2188.9 59.1 %collective-permute-start.12 = (bf16[256,3584]{1,0:T(8,128)(2,1)}, bf16[256,3584]{1,0:T(8,128)(2,1)}, u32[]{:S(2)}, u32[]{:S(2)}) collective-permute-start(bf16[256,3584]{1,0:T(8,128)(2,1)} %collective-permute-done.11), channel_id=1, source_target_pairs={{0,2},{2,4},{4,6},{6,8},{8,10},{10,12},{12,14},{14,16},{16,18},{18... | collective-permute-start | bytes 5505032 | tf_op jit(solution)/shard_map/ppermute | solution.py:18
  2248.0 43.5 %collective-permute-start.13 = (bf16[256,3584]{1,0:T(8,128)(2,1)}, bf16[256,3584]{1,0:T(8,128)(2,1)}, u32[]{:S(2)}, u32[]{:S(2)}) collective-permute-start(bf16[256,3584]{1,0:T(8,128)(2,1)} %collective-permute-done.12), channel_id=1, source_target_pairs={{0,2},{2,4},{4,6},{6,8},{8,10},{10,12},{12,14},{14,16},{16,18},{18... | collective-permute-start | bytes 5505032 | tf_op jit(solution)/shard_map/ppermute | solution.py:18
  2291.5 25.2 %collective-permute-start.14 = (bf16[256,3584]{1,0:T(8,128)(2,1)}, bf16[256,3584]{1,0:T(8,128)(2,1)S(1)}, u32[]{:S(2)}, u32[]{:S(2)}) collective-permute-start(bf16[256,3584]{1,0:T(8,128)(2,1)} %collective-permute-done.13), channel_id=1, source_target_pairs={{0,2},{2,4},{4,6},{6,8},{8,10},{10,12},{12,14},{14,16},{16,18},{18... | collective-permute-start | bytes 5505032 | tf_op jit(solution)/shard_map/ppermute | solution.py:18
  (390 other events, 961.7 us)
Sparse Core Ops, SparseCore 0:
  10.1 128.2 all-gather.2
  2264.9 11.7 all-gather.4
